TPU v7x, 32 devices: a whole 2x2x4 slice. The times are simulated.
32 devices in a mesh: prow: 8 (over z, y), pcol: 4 (over x, core).
Axes of the slice: x: 2, y: 2, z: 4, core: 2. Of those that a mesh axis runs over, the one named last changes fastest.
Arguments:
- paper_x: bfloat16 [8192, 768], P(('prow', 'pcol')), may hold values from -6 to 6
- author_x: bfloat16 [4096, 768], P(('pcol', 'prow')), may hold values from -6 to 6
- w_self: bfloat16 [768, 768], replicated, may hold values from -0.21875 to 0.21875
- w_rel: bfloat16 [2, 768, 768], replicated, may hold values from -0.009765625 to 0.009765625
- w_two: bfloat16 [768, 768], replicated, may hold values from -0.0068359375 to 0.0068359375
- block_rows: int32 [8, 4, 32], P('prow', 'pcol'), may hold values from 0 to 7, as said below
- block_cols: int32 [8, 4, 32], P('prow', 'pcol'), may hold values from 0 to 7, as said below
- block_type: int32 [8, 4, 32], P('prow', 'pcol'), may hold values from 0 to 1
- block_count: int32 [8, 4], P('prow', 'pcol'), may hold values from 8 to 32, as said below
- block_vals: bfloat16 [8, 4, 32, 128, 128], P('prow', 'pcol'), may hold values from 0 to 1, as said below
Outputs:
- paper_hidden: bfloat16 [8192, 768], P(('prow', 'pcol'))
- author_out: bfloat16 [4096, 768], P(('pcol', 'prow'))
Inputs may be any that keep to these rules, and one draw needn't show every extreme that they name: `block_rows`: within one tile the live and dead slots name distinct positions; block rows are below 8. `block_cols`: block columns are below 8; with block_rows, positions of one tile are distinct. `block_count`: slots 0 to count - 1 of a tile are live; some tile holds 32 live slots and some tile 32 // 4 in every draw. `block_vals`: every entry is 0 or 1.
All inputs are finite; a program needn't handle non-finite values.
Results may differ from a plain program's by a relative error of at most 0.0041.
Values may be sent and summed in bfloat16 or wider, within the bound.
A program may use at most 64 MiB of HBM per device.

v0:
```python
import functools

import jax
import jax.numpy as jnp
from jax import lax
from jax.experimental import pallas as pl
from jax.experimental.pallas import tpu as pltpu
from jax.sharding import PartitionSpec as P

MESH = pl.DeviceIdType.MESH
F32 = jnp.float32
BF16 = jnp.bfloat16


def dot(a, b):
    return jnp.dot(a, b, preferred_element_type=F32)


def kernel(
    n_prow, n_pcol, tile,
    tab, author, paper_h, w_self_h, w_rel_h, w_two_h, blocks_h,
    hidden, author_out,
    paper, w_self, w_rel, w_two, blocks,
    x_all, msgs, dense, dense_t, self_term,
    pair_out, pair_in, x_out, x_in, acc,
    rows_all, y_out, y_in, y_acc, z_out, z_in,
    local_sem,
    g_send, g_recv, gy_send, gy_recv,
    pair_s, pair_r, xs, xr,
    o_send, o_recv, oc_send, oc_recv,
    ys, yr, zs, zr,
):
    i = lax.axis_index("prow")
    j = lax.axis_index("pcol")
    z, y = i // 2, i % 2
    x, c = j // 2, j % 2
    H, G = n_prow // 2, n_pcol // 2
    own_papers, width = paper.shape
    own_authors = author.shape[0]
    side = blocks.shape[1]
    authors = own_authors * n_prow
    papers = own_papers * n_pcol
    nf = width // tile
    y_part = z * 2 + 1 - y
    c_part = x * 2 + 1 - c

    waits = []

    def send(cond, src, dst, ss, rs, di, dj):
        def desc():
            return pltpu.make_async_remote_copy(
                src_ref=src, dst_ref=dst, send_sem=ss, recv_sem=rs,
                device_id=(di, dj), device_id_type=MESH,
            )

        if cond is None:
            desc().start()
        else:
            @pl.when(cond)
            def _():
                desc().start()
        waits.append((cond, desc))

    def arrive(dst, ss, rs):
        pltpu.make_async_remote_copy(
            src_ref=dst, dst_ref=dst, send_sem=ss, recv_sem=rs,
            device_id=(i, c_part), device_id_type=MESH,
        ).wait_recv()

    loads = [
        pltpu.make_async_copy(src, dst, local_sem.at[n])
        for n, (src, dst) in enumerate(
            ((blocks_h, blocks), (w_rel_h, w_rel), (paper_h, paper), (w_self_h, w_self), (w_two_h, w_two))
        )
    ]
    for load in loads:
        load.start()

    barrier = pltpu.get_barrier_semaphore()

    def greet(cond, di, dj):
        def go():
            pl.semaphore_signal(barrier, inc=1, device_id=(di, dj), device_id_type=MESH)

        if cond is None:
            go()
        else:
            pl.when(cond)(go)

    up_z, down_z, up_x, down_x = z < H - 1, z > 0, x < G - 1, x > 0
    greet(None, y_part, j)
    greet(None, i, c_part)
    greet(up_z, i + 2, j)
    greet(down_z, i - 2, j)
    greet(up_x, i, j + 2)
    greet(down_x, i, j - 2)
    peers = 2
    for cond in (up_z, down_z, up_x, down_x):
        peers = peers + cond.astype(jnp.int32)
    pl.semaphore_wait(barrier, peers)

    parts = g_send.shape[2]
    part_rows = own_authors // parts

    def piece(zz, yy, h):
        return x_all.at[zz, yy, pl.ds(h * part_rows, part_rows), :]

    for h in range(parts):
        mine = author.at[pl.ds(h * part_rows, part_rows), :]
        send(up_z, mine, piece(z, y, h), g_send.at[0, 0, h], g_recv.at[0, 0, h], i + 2, j)
        send(down_z, mine, piece(z, y, h), g_send.at[1, 0, h], g_recv.at[1, 0, h], i - 2, j)
        send(None, mine, piece(z, y, h), gy_send.at[2, 0, h], gy_recv.at[2, 0, h], y_part, j)
    x_all[z, y] = author[...]

    loads[0].wait()
    row_blocks, col_blocks = papers // side, authors // side
    p_step, a_step = min(side, own_papers), min(side, own_authors)

    def densify(first, last):
        for rb in range(first, last):
            for cb in range(col_blocks):
                pos = rb * col_blocks + cb
                slot, kind = tab[0, pos], tab[1, pos]
                block = blocks[slot].astype(F32)
                for t in range(2):
                    part = (block * (kind == t).astype(F32)).astype(BF16)
                    lo = t * authors + cb * side
                    for sub in range(side // p_step):
                        row = rb * side + sub * p_step
                        dense[row // own_papers, row % own_papers:row % own_papers + p_step, lo:lo + side] = part[
                            sub * p_step:(sub + 1) * p_step
                        ]
                flip = (block * (kind < 2).astype(F32)).T.astype(BF16)
                for sub in range(side // a_step):
                    owner = (cb * side + sub * a_step) // own_authors
                    dense_t[owner % 2, owner // 2, :, rb * side:(rb + 1) * side] = flip[sub * a_step:(sub + 1) * a_step]

    def message_pair(zz):
        pair = x_all[zz].reshape(2 * own_authors, width)
        for t in range(2):
            @pl.loop(0, nf)
            def _(n):
                cols = pl.ds(pl.multiple_of(n * tile, tile), tile)
                msgs[t, zz, :, cols] = dot(pair, w_rel[t, :, cols]).astype(BF16)

    def z_arrival(s):
        for h in range(parts):
            for way, near, inside, more, to in (
                (0, z - 1 - s, z - 1 - s >= 0, up_z, i + 2),
                (1, z + 1 + s, z + 1 + s <= H - 1, down_z, i - 2),
            ):
                part = piece(near, y, h)

                @pl.when(inside)
                def _():
                    arrive(part, g_send.at[way, s, h], g_recv.at[way, s, h])

                if s + 1 <= H - 2:
                    send(inside & more, part, part, g_send.at[way, s + 1, h], g_recv.at[way, s + 1, h], to, j)
                send(inside, part, part, gy_send.at[way, s, h], gy_recv.at[way, s, h], y_part, j)

    def y_arrival(s):
        for way, near, inside in ((0, z - 1 - s, z - 1 - s >= 0), (1, z + 1 + s, z + 1 + s <= H - 1)):
            @pl.when(inside)
            def _():
                for h in range(parts):
                    arrive(piece(near, 1 - y, h), gy_send.at[way, s, h], gy_recv.at[way, s, h])
                message_pair(near)

    densify(0, row_blocks // 2)
    z_arrival(0)
    densify(row_blocks // 2, row_blocks)
    if H > 2:
        z_arrival(1)
    loads[2].wait()
    loads[3].wait()
    for f in range(nf):
        cols = slice(f * tile, (f + 1) * tile)
        self_term[:, cols] = dot(paper[...], w_self[:, cols])
    loads[1].wait()
    loads[4].wait()
    for h in range(parts):
        arrive(piece(z, 1 - y, h), gy_send.at[2, 0, h], gy_recv.at[2, 0, h])
    message_pair(z)
    for s in range(2, H - 1):
        z_arrival(s)
        y_arrival(s - 2)
    for s in range(max(H - 3, 0), H - 1):
        y_arrival(s)

    def first_hop(q, f):
        cols = slice(f * tile, (f + 1) * tile)
        return dot(dense[q], msgs[:, :, :, cols].reshape(2 * authors, tile))

    for d in range(1, G + 1):
        b = lax.rem(x + d, G)
        for f in range(nf):
            pair_out[d - 1, f] = first_hop(b * 2 + 1 - c, f).astype(BF16)
            send(None, pair_out.at[d - 1, f], pair_in.at[d - 1, f], pair_s.at[d - 1, f], pair_r.at[d - 1, f], i, c_part)
        for f in range(nf):
            acc[f] = first_hop(b * 2 + c, f)
            arrive(pair_in.at[d - 1, f], pair_s.at[d - 1, f], pair_r.at[d - 1, f])
            acc[f] = acc[f] + pair_in[d - 1, f].astype(F32)
            if d == G:
                continue
            is_up, is_down = b > x, b < x

            @pl.when(is_up & (x > 0))
            def _():
                arrive(x_in.at[0, b, f], xs.at[0, b, f], xr.at[0, b, f])
                acc[f] = acc[f] + x_in[0, b, f].astype(F32)

            @pl.when(is_down & (x < G - 1))
            def _():
                arrive(x_in.at[1, b, f], xs.at[1, b, f], xr.at[1, b, f])
                acc[f] = acc[f] + x_in[1, b, f].astype(F32)

            x_out[d - 1, f] = acc[f].astype(BF16)
            send(is_up, x_out.at[d - 1, f], x_in.at[0, b, f], xs.at[0, b, f], xr.at[0, b, f], i, j + 2)
            send(is_down, x_out.at[d - 1, f], x_in.at[1, b, f], xs.at[1, b, f], xr.at[1, b, f], i, j - 2)

    for f in range(nf):
        cols = slice(f * tile, (f + 1) * tile)

        @pl.when(x > 0)
        def _():
            arrive(x_in.at[0, x, f], xs.at[0, x, f], xr.at[0, x, f])
            acc[f] = acc[f] + x_in[0, x, f].astype(F32)

        @pl.when(x < G - 1)
        def _():
            arrive(x_in.at[1, x, f], xs.at[1, x, f], xr.at[1, x, f])
            acc[f] = acc[f] + x_in[1, x, f].astype(F32)

        hidden[:, cols] = jnp.maximum(acc[f] + self_term[:, cols], 0.0).astype(BF16)

    for f in range(nf):
        cols = slice(f * tile, (f + 1) * tile)
        rows_all[f, x, c] = dot(hidden[...], w_two[:, cols]).astype(BF16)
        own = rows_all.at[f, x, c]
        send(up_x, own, own, o_send.at[0, 0, f], o_recv.at[0, 0, f], i, j + 2)
        send(down_x, own, own, o_send.at[1, 0, f], o_recv.at[1, 0, f], i, j - 2)
        send(None, own, own, oc_send.at[2, 0, f], oc_recv.at[2, 0, f], i, c_part)

    def pass_on(f):
        for s in range(G - 1):
            below, above = x - 1 - s, x + 1 + s

            @pl.when(below >= 0)
            def _():
                arrive(rows_all.at[f, below, c], o_send.at[0, s, f], o_recv.at[0, s, f])

            part = rows_all.at[f, below, c]
            if s + 1 <= G - 2:
                send((below >= 0) & up_x, part, part, o_send.at[0, s + 1, f], o_recv.at[0, s + 1, f], i, j + 2)
            send(below >= 0, part, part, oc_send.at[0, s, f], oc_recv.at[0, s, f], i, c_part)

            @pl.when(above <= G - 1)
            def _():
                arrive(rows_all.at[f, above, c], o_send.at[1, s, f], o_recv.at[1, s, f])

            part = rows_all.at[f, above, c]
            if s + 1 <= G - 2:
                send((above <= G - 1) & down_x, part, part, o_send.at[1, s + 1, f], o_recv.at[1, s + 1, f], i, j - 2)
            send(above <= G - 1, part, part, oc_send.at[1, s, f], oc_recv.at[1, s, f], i, c_part)

    def collect(f):
        arrive(rows_all.at[f, x, 1 - c], oc_send.at[2, 0, f], oc_recv.at[2, 0, f])
        for s in range(G - 1):
            below, above = x - 1 - s, x + 1 + s

            @pl.when(below >= 0)
            def _():
                arrive(rows_all.at[f, below, 1 - c], oc_send.at[0, s, f], oc_recv.at[0, s, f])

            @pl.when(above <= G - 1)
            def _():
                arrive(rows_all.at[f, above, 1 - c], oc_send.at[1, s, f], oc_recv.at[1, s, f])

    low = z < H // 2
    for f in range(nf):
        pass_on(f)
        collect(f)
        table = rows_all[f].reshape(papers, tile)
        far = dot(dense_t[1 - y].reshape(H * own_authors, papers), table)
        y_out[f] = far.astype(BF16).reshape(H, own_authors, tile)
        for s in range(H - 1):
            for b, cond in ((H - 1 - s, (z < H - 1 - s) & low), (s, z > s), (H - 1 - s, (z < H - 1 - s) & (z >= H // 2))):
                send(cond, y_out.at[f, b], y_in.at[f, b], ys.at[f, b], yr.at[f, b], y_part, j)
        near = dot(dense_t[y].reshape(H * own_authors, papers), table)
        y_acc[f] = near.reshape(H, own_authors, tile)
    for f in range(nf):
        send(None, y_out.at[f, z], y_in.at[f, z], ys.at[f, z], yr.at[f, z], y_part, j)

    for f in range(nf):
        for s in range(H - 1):
            for way, b, cond in (
                (0, H - 1 - s, (z < H - 1 - s) & low), (1, s, z > s), (0, H - 1 - s, (z < H - 1 - s) & (z >= H // 2))
            ):
                first = (z == 0) if way == 0 else (z == H - 1)

                @pl.when(cond)
                def _():
                    arrive(y_in.at[f, b], ys.at[f, b], yr.at[f, b])
                    y_acc[f, b] = y_acc[f, b] + y_in[f, b].astype(F32)

                @pl.when(cond & jnp.logical_not(first))
                def _():
                    arrive(z_in.at[way, f, b], zs.at[way, f, b], zr.at[way, f, b])
                    y_acc[f, b] = y_acc[f, b] + z_in[way, f, b].astype(F32)

                @pl.when(cond)
                def _():
                    z_out[way, f, b] = y_acc[f, b].astype(BF16)

                send(cond, z_out.at[way, f, b], z_in.at[way, f, b], zs.at[way, f, b], zr.at[way, f, b],
                     i + 2 if way == 0 else i - 2, j)

    for f in range(nf):
        cols = slice(f * tile, (f + 1) * tile)
        total = y_acc.at[f, z]
        arrive(y_in.at[f, z], ys.at[f, z], yr.at[f, z])
        total[...] = total[...] + y_in[f, z].astype(F32)

        @pl.when(z > 0)
        def _():
            arrive(z_in.at[0, f, z], zs.at[0, f, z], zr.at[0, f, z])
            total[...] = total[...] + z_in[0, f, z].astype(F32)

        @pl.when(z < H - 1)
        def _():
            arrive(z_in.at[1, f, z], zs.at[1, f, z], zr.at[1, f, z])
            total[...] = total[...] + z_in[1, f, z].astype(F32)

        author_out[:, cols] = total[...].astype(BF16)

    for cond, desc in waits:
        if cond is None:
            desc().wait_send()
        else:
            @pl.when(cond)
            def _():
                desc().wait_send()


def per_device(
    n_prow, n_pcol, paper_x, author_x, w_self, w_rel, w_two,
    block_rows, block_cols, block_type, block_count, block_vals,
):
    slots, side = block_vals.shape[2], block_vals.shape[3]
    own_papers, width = paper_x.shape
    own_authors = author_x.shape[0]
    papers, authors = own_papers * n_pcol, own_authors * n_prow
    col_blocks = authors // side
    places = (papers // side) * col_blocks
    H, G = n_prow // 2, n_pcol // 2
    tile = 256 if width % 256 == 0 else 128
    nf = width // tile

    slot = jnp.arange(slots, dtype=jnp.int32)
    where = block_rows.reshape(slots) * col_blocks + block_cols.reshape(slots)
    live = slot < block_count.reshape(())
    hit = (where[:, None] == jnp.arange(places, dtype=jnp.int32)[None, :]) & live[:, None]
    which = jnp.sum(jnp.where(hit, slot[:, None], 0), axis=0)
    kind = 2 + jnp.sum(jnp.where(hit, block_type.reshape(slots)[:, None] - 2, 0), axis=0)
    tab = jnp.stack([which, kind]).astype(jnp.int32)

    vmem, anyspace, smem = pltpu.VMEM, pl.ANY, pltpu.SMEM
    dma = pltpu.SemaphoreType.DMA
    hz, gx = max(H - 1, 1), max(G - 1, 1)
    return pl.pallas_call(
        functools.partial(kernel, n_prow, n_pcol, tile),
        out_shape=(
            jax.ShapeDtypeStruct((own_papers, width), BF16),
            jax.ShapeDtypeStruct((own_authors, width), BF16),
        ),
        in_specs=[pl.BlockSpec(memory_space=smem), pl.BlockSpec(memory_space=vmem)]
        + [pl.BlockSpec(memory_space=anyspace)] * 5,
        out_specs=(pl.BlockSpec(memory_space=vmem),) * 2,
        scratch_shapes=[
            vmem((own_papers, width), BF16),
            vmem((width, width), BF16),
            vmem(w_rel.shape, BF16),
            vmem((width, width), BF16),
            vmem((slots, side, side), BF16),
            vmem((H, 2, own_authors, width), BF16),
            vmem((2, H, 2 * own_authors, width), BF16),
            vmem((n_pcol, own_papers, 2 * authors), BF16),
            vmem((2, H, own_authors, papers), BF16),
            vmem((own_papers, width), F32),
            vmem((G, nf, own_papers, tile), BF16),
            vmem((G, nf, own_papers, tile), BF16),
            vmem((gx, nf, own_papers, tile), BF16),
            vmem((2, G, nf, own_papers, tile), BF16),
            vmem((nf, own_papers, tile), F32),
            vmem((nf, G, 2, own_papers, tile), BF16),
            vmem((nf, H, own_authors, tile), BF16),
            vmem((nf, H, own_authors, tile), BF16),
            vmem((nf, H, own_authors, tile), F32),
            vmem((2, nf, H, own_authors, tile), BF16),
            vmem((2, nf, H, own_authors, tile), BF16),
            dma((5,)),
            dma((2, hz, 2)), dma((2, hz, 2)), dma((3, hz, 2)), dma((3, hz, 2)),
            dma((G, nf)), dma((G, nf)), dma((2, G, nf)), dma((2, G, nf)),
            dma((2, gx, nf)), dma((2, gx, nf)), dma((3, gx, nf)), dma((3, gx, nf)),
            dma((nf, H)), dma((nf, H)), dma((2, nf, H)), dma((2, nf, H)),
        ],
        compiler_params=pltpu.CompilerParams(
            collective_id=0, has_side_effects=True, vmem_limit_bytes=60 * 1024 * 1024
        ),
    )(tab, author_x, paper_x, w_self, w_rel, w_two, block_vals.reshape(slots, side, side))


def solution(mesh):
    return jax.shard_map(
        functools.partial(per_device, mesh.shape["prow"], mesh.shape["pcol"]),
        mesh=mesh,
        in_specs=(
            P(("prow", "pcol"), None),
            P(("pcol", "prow"), None),
            P(),
            P(),
            P(),
            P("prow", "pcol", None),
            P("prow", "pcol", None),
            P("prow", "pcol", None),
            P("prow", "pcol"),
            P("prow", "pcol", None, None, None),
        ),
        out_specs=(P(("prow", "pcol"), None), P(("pcol", "prow"), None)),
        check_vma=False,
    )
```

profile of v0, /device:TPU:0, one launch (start us, length us, event | category | flops | bytes accessed | tf_op | source)
XLA Modules:
  0.0 79.4 jit_solution(221966270112591688)
XLA Ops:
  1.3 0.7 add_bitcast_fusion.1
  2.0 0.1 select_reduce_fusion.1
  2.1 0.6 pad_add_fusion.tab
  2.7 73.3 %shard_map.113 = (bf16[256,768]{1,0:T(8,128)(2,1)}, bf16[128,768]{1,0:T(8,128)(2,1)}) custom-call(s32[2,64]{1,0:T(2,128)} %pad_add_fusion.tab, bf16[128,768]{1,0:T(8,128)(2,1)} %author.1, bf16[256,768]{1,0:T(8,128)(2,1)} %paper_h.1, bf16[768,768]{1,0:T(8,128)(2,1)} %w_self_h.1, bf16[2,768,768]{2,1,0:T(8,128)(2,1)} %w_rel_h.1, bf16[768,768]{1,0:T(8,128)(2,1)} %w_two_h.1, ...), custom_call_target="tpu_custom_call" | custom-call | tf_op jit(solution)/shard_map/pallas_call | solution.py:371
  76.0 1.8 %copy.15 = bf16[256,768]{1,0:T(8,128)(2,1)} copy(bf16[256,768]{1,0:T(8,128)(2,1)} %get-tuple-element.8) | data formatting | bytes 786432
  77.8 1.6 %copy.16 = bf16[128,768]{1,0:T(8,128)(2,1)} copy(bf16[128,768]{1,0:T(8,128)(2,1)} %get-tuple-element.9) | data formatting | bytes 393216
  (2 shorter events, 0.0 us)
where the time goes:
time: 79.6 us; the launch traced here: 79.4 us
  Pallas kernels  73.3 us (92%)
  local copies, waits for them, and re-layouts  3.38 us (4%)
  other arithmetic  1.37 us (2%)
  between operations  1.3 us (2%)
    pallas_call x1, Pallas kernels, per_device(): pl.pallas_call(functools.partial(kernel, n_prow, n_pcol, tile), out_shape...  73.3 us
    unnamed x2, local copies, waits for them, and re-layouts  3.38 us

commit v1 on v0

v1 whole, which is shorter than its diff:
```python
import functools

import jax
import jax.numpy as jnp
from jax import lax
from jax.experimental import pallas as pl
from jax.experimental.pallas import tpu as pltpu
from jax.sharding import PartitionSpec as P

MESH = pl.DeviceIdType.MESH
F32 = jnp.float32
BF16 = jnp.bfloat16


def dot(a, b):
    return jnp.dot(a, b, preferred_element_type=F32)


def kernel(
    n_prow, n_pcol, wide, fc,
    tab, author_h, paper_h, w_self_h, w_rel_h, w_two_h, blocks_h,
    hidden_h, author_out,
    paper, w_self, w_rel, w_two, blocks,
    x_all, msgs, dense, dense_t, acc,
    pair_out, pair_in, x_out, x_in, h_all, hidden,
    y_out, y_in, y_acc, z_out, z_in, out_acc,
    local_sem,
    g_send, g_recv, gy_send, gy_recv,
    pair_s, pair_r, xs, xr, hs, hr,
    ys, yr, zs, zr,
):
    i = lax.axis_index("prow")
    j = lax.axis_index("pcol")
    z, y = i // 2, i % 2
    x, c = j // 2, j % 2
    H, G = n_prow // 2, n_pcol // 2
    own_papers, width = paper.shape
    own_authors = author_h.shape[0]
    side = blocks.shape[1]
    authors = own_authors * n_prow
    papers = own_papers * n_pcol
    pair_authors = 2 * own_authors
    nf, nb = width // fc, width // wide
    per = wide // fc
    y_part = z * 2 + 1 - y
    c_part = x * 2 + 1 - c
    low = z < H // 2

    waits = []

    def send(cond, src, dst, ss, rs, di, dj):
        def desc():
            return pltpu.make_async_remote_copy(
                src_ref=src, dst_ref=dst, send_sem=ss, recv_sem=rs,
                device_id=(di, dj), device_id_type=MESH,
            )

        if cond is None:
            desc().start()
        else:
            @pl.when(cond)
            def _():
                desc().start()
        waits.append((cond, desc))

    def arrive(dst, ss, rs):
        pltpu.make_async_remote_copy(
            src_ref=dst, dst_ref=dst, send_sem=ss, recv_sem=rs,
            device_id=(i, c_part), device_id_type=MESH,
        ).wait_recv()

    barrier = pltpu.get_barrier_semaphore()

    def greet(cond, di, dj):
        def go():
            pl.semaphore_signal(barrier, inc=1, device_id=(di, dj), device_id_type=MESH)

        if cond is None:
            go()
        else:
            pl.when(cond)(go)

    up_z, down_z = z < H - 1, z > 0
    greet(up_z, i + 2, j)
    greet(down_z, i - 2, j)
    greet(None, y_part, j)
    for d in range(1, G):
        greet(None, i, lax.rem(x + d, G) * 2 + c)
    greet(None, i, c_part)
    for d in range(2, H):
        greet(z + d <= H - 1, i + 2 * d, j)
        greet(z - d >= 0, i - 2 * d, j)

    loads = [
        pltpu.make_async_copy(src, dst, local_sem.at[n])
        for n, (src, dst) in enumerate(
            (
                (blocks_h, blocks), (w_rel_h, w_rel), (paper_h, paper), (w_self_h, w_self), (w_two_h, w_two),
                (author_h, x_all.at[z, y]),
            )
        )
    ]
    for load in loads:
        load.start()

    pl.semaphore_wait(barrier, 1 + G + H - 1)

    parts = g_send.shape[2]
    part_rows = own_authors // parts

    def piece(zz, yy, h):
        return x_all.at[zz, yy, pl.ds(h * part_rows, part_rows), :]

    for h in range(parts):
        mine = author_h.at[pl.ds(h * part_rows, part_rows), :]
        send(up_z, mine, piece(z, y, h), g_send.at[0, 0, h], g_recv.at[0, 0, h], i + 2, j)
        send(down_z, mine, piece(z, y, h), g_send.at[1, 0, h], g_recv.at[1, 0, h], i - 2, j)
        send(None, mine, piece(z, y, h), gy_send.at[2, 0, h], gy_recv.at[2, 0, h], y_part, j)

    loads[0].wait()
    row_blocks, col_blocks = papers // side, authors // side
    p_step, a_step, pair_step = min(side, own_papers), min(side, own_authors), min(side, pair_authors)

    def densify(first, last):
        for rb in range(first, last):
            for cb in range(col_blocks):
                pos = rb * col_blocks + cb
                slot, kind = tab[0, pos], tab[1, pos]
                block = blocks[slot].astype(F32)
                for t in range(2):
                    part = (block * (kind == t).astype(F32)).astype(BF16)
                    for sub in range(side // p_step):
                        row = rb * side + sub * p_step
                        for lane in range(side // pair_step):
                            col = cb * side + lane * pair_step
                            lo = t * pair_authors + col % pair_authors
                            dense[
                                col // pair_authors, row // own_papers,
                                row % own_papers:row % own_papers + p_step, lo:lo + pair_step,
                            ] = part[sub * p_step:(sub + 1) * p_step, lane * pair_step:(lane + 1) * pair_step]
                flip = (block * (kind < 2).astype(F32)).T.astype(BF16)
                for sub in range(side // a_step):
                    owner = (cb * side + sub * a_step) // own_authors
                    dense_t[owner % 2, owner // 2, :, rb * side:(rb + 1) * side] = flip[sub * a_step:(sub + 1) * a_step]

    def z_arrival(s):
        for h in range(parts):
            for way, near, inside, more, to in (
                (0, z - 1 - s, z - 1 - s >= 0, up_z, i + 2),
                (1, z + 1 + s, z + 1 + s <= H - 1, down_z, i - 2),
            ):
                part = piece(near, y, h)

                @pl.when(inside)
                def _():
                    arrive(part, g_send.at[way, s, h], g_recv.at[way, s, h])

                if s + 1 <= H - 2:
                    send(inside & more, part, part, g_send.at[way, s + 1, h], g_recv.at[way, s + 1, h], to, j)
                send(inside, part, part, gy_send.at[way, s, h], gy_recv.at[way, s, h], y_part, j)

    def messages(zz, n):
        pair = x_all[zz].reshape(pair_authors, width)
        cols = slice(n * wide, (n + 1) * wide)
        for t in range(2):
            msgs[zz, t * pair_authors:(t + 1) * pair_authors, cols] = dot(pair, w_rel[t, :, cols]).astype(BF16)

    def hop_one(zz, n, b, cc, first):
        part = dot(dense[zz, b * 2 + cc], msgs[zz, :, n * wide:(n + 1) * wide])
        for p in range(per):
            value = part[:, p * fc:(p + 1) * fc]
            f = n * per + p
            acc[f, b, cc] = value if first else acc[f, b, cc] + value

    def slab(zz, first):
        for n in range(nb):
            messages(zz, n)
            for b in range(G):
                for cc in range(2):
                    hop_one(zz, n, b, cc, first)

    reach = jnp.minimum(z, H - 1 - z)

    def order(k):
        both = k < 2 * reach
        dist = jnp.where(both, k // 2 + 1, k - reach + 1)
        above = jnp.where(both, k % 2 == 0, low)
        return dist, above.astype(jnp.int32), jnp.where(above, z + dist, z - dist)

    def from_y(k):
        dist, way, near = order(k)
        for h in range(parts):
            arrive(piece(near, 1 - y, h), gy_send.at[way, dist - 1, h], gy_recv.at[way, dist - 1, h])
        return near

    half = row_blocks // 2
    densify(0, half)
    z_arrival(0)
    densify(half, row_blocks)
    for load in loads[1:]:
        load.wait()
    for h in range(parts):
        arrive(piece(z, 1 - y, h), gy_send.at[2, 0, h], gy_recv.at[2, 0, h])
    slab(z, True)
    for n in range(nb):
        cols = slice(n * wide, (n + 1) * wide)
        own = dot(paper[...], w_self[:, cols])
        for p in range(per):
            f = n * per + p
            acc[f, x, c] = acc[f, x, c] + own[:, p * fc:(p + 1) * fc]
    if H > 2:
        z_arrival(1)
    for k in range(H - 2):
        slab(from_y(k), False)
        if k + 2 <= H - 2:
            z_arrival(k + 2)
    last = from_y(H - 2)

    def to_pair(n):
        messages(last, n)
        for b in range(G):
            hop_one(last, n, b, 1 - c, False)
        for p in range(per):
            f = n * per + p
            for b in range(G):
                pair_out[f, b] = acc[f, b, 1 - c].astype(BF16)
            send(None, pair_out.at[f], pair_in.at[f], pair_s.at[f], pair_r.at[f], i, c_part)
        for b in range(G):
            hop_one(last, n, b, c, False)

    def to_x(f):
        arrive(pair_in.at[f], pair_s.at[f], pair_r.at[f])
        for b in range(G):
            total = acc[f, b, c] + pair_in[f, b].astype(F32)
            acc[f, b, c] = total
            x_out[f, b] = total.astype(BF16)
        for d in range(1, G):
            send(None, x_out.at[f], x_in.at[d - 1, f], xs.at[d - 1, f], xr.at[d - 1, f],
                 i, lax.rem(x + d, G) * 2 + c)

    def from_x(f):
        for d in range(1, G):
            arrive(x_in.at[d - 1, f], xs.at[d - 1, f], xr.at[d - 1, f])
        for b in range(G):
            total = acc[f, b, c]
            for d in range(1, G):
                total = total + x_in[d - 1, f, b].astype(F32)
            h_all[f, c, b] = jnp.maximum(total, 0.0).astype(BF16)
        send(None, h_all.at[f, c], h_all.at[f, c], hs.at[f], hr.at[f], i, c_part)
        hidden[:, f * fc:(f + 1) * fc] = h_all[f, c, x]

    def target(k):
        return jnp.where(low, H - 1 - k, k)

    def to_y(f):
        arrive(h_all.at[f, 1 - c], hs.at[f], hr.at[f])
        table = jnp.concatenate(
            [h_all[f, q % 2, q // 2] for q in range(n_pcol)], axis=0
        )
        far = dot(dense_t[1 - y].reshape(H * own_authors, papers), table)
        y_out[f] = far.astype(BF16).reshape(H, own_authors, fc)
        for k in range(H):
            b = target(k)
            send(None, y_out.at[f, b], y_in.at[f, b], ys.at[f, b], yr.at[f, b], y_part, j)
        near = dot(dense_t[y].reshape(H * own_authors, papers), table)
        y_acc[f] = near.reshape(H, own_authors, fc)

    def to_z(f):
        for k in range(H):
            b = target(k)
            arrive(y_in.at[f, b], ys.at[f, b], yr.at[f, b])
            total = y_acc[f, b] + y_in[f, b].astype(F32)
            y_acc[f, b] = total
            z_out[f, b] = total.astype(BF16)
            send(b != z, z_out.at[f, b], z_in.at[f, z], zs.at[f, b], zr.at[f, z], b * 2 + y, j)

    def finish(f):
        for s in range(H):
            @pl.when(z != s)
            def _():
                arrive(z_in.at[f, s], zs.at[f, s], zr.at[f, s])
                y_acc[f, z] = y_acc[f, z] + z_in[f, s].astype(F32)

        total = y_acc[f, z]
        high = total.astype(BF16)
        rest = (total - high.astype(F32)).astype(BF16)
        for n in range(nb):
            cols = slice(n * wide, (n + 1) * wide)
            weight = w_two[f * fc:(f + 1) * fc, cols]
            value = dot(high, weight) + dot(rest, weight)
            out_acc[:, cols] = value if f == 0 else out_acc[:, cols] + value

    for n in range(nb):
        to_pair(n)
        if n > 0:
            for p in range(per):
                to_x((n - 1) * per + p)
    for p in range(per):
        to_x((nb - 1) * per + p)

    for f in range(nf):
        from_x(f)
        to_y(f)
        if f >= 1:
            to_z(f - 1)
        if f >= 4:
            finish(f - 4)
    store = pltpu.make_async_copy(hidden, hidden_h, local_sem.at[0])
    store.start()
    for f in range(max(nf - 4, 0), nf - 2):
        finish(f)
    to_z(nf - 1)
    for f in range(max(nf - 2, 0), nf):
        finish(f)
    author_out[...] = out_acc[...].astype(BF16)
    store.wait()

    for cond, desc in waits:
        if cond is None:
            desc().wait_send()
        else:
            @pl.when(cond)
            def _():
                desc().wait_send()


def per_device(
    n_prow, n_pcol, paper_x, author_x, w_self, w_rel, w_two,
    block_rows, block_cols, block_type, block_count, block_vals,
):
    slots, side = block_vals.shape[2], block_vals.shape[3]
    own_papers, width = paper_x.shape
    own_authors = author_x.shape[0]
    papers, authors = own_papers * n_pcol, own_authors * n_prow
    col_blocks = authors // side
    places = (papers // side) * col_blocks
    H, G = n_prow // 2, n_pcol // 2
    wide = 256 if width % 256 == 0 else 128
    fc = 128
    nf = width // fc

    slot = jnp.arange(slots, dtype=jnp.int32)
    where = block_rows.reshape(slots) * col_blocks + block_cols.reshape(slots)
    live = slot < block_count.reshape(())
    hit = (where[:, None] == jnp.arange(places, dtype=jnp.int32)[None, :]) & live[:, None]
    which = jnp.sum(jnp.where(hit, slot[:, None], 0), axis=0)
    kind = 2 + jnp.sum(jnp.where(hit, block_type.reshape(slots)[:, None] - 2, 0), axis=0)
    tab = jnp.stack([which, kind]).astype(jnp.int32)

    vmem, anyspace, smem = pltpu.VMEM, pl.ANY, pltpu.SMEM
    dma = pltpu.SemaphoreType.DMA
    hz, gx = max(H - 1, 1), max(G - 1, 1)
    return pl.pallas_call(
        functools.partial(kernel, n_prow, n_pcol, wide, fc),
        out_shape=(
            jax.ShapeDtypeStruct((own_papers, width), BF16),
            jax.ShapeDtypeStruct((own_authors, width), BF16),
        ),
        in_specs=[pl.BlockSpec(memory_space=smem)]
        + [pl.BlockSpec(memory_space=anyspace)] * 6,
        out_specs=(pl.BlockSpec(memory_space=anyspace), pl.BlockSpec(memory_space=vmem)),
        scratch_shapes=[
            vmem((own_papers, width), BF16),
            vmem((width, width), BF16),
            vmem(w_rel.shape, BF16),
            vmem((width, width), BF16),
            vmem((slots, side, side), BF16),
            vmem((H, 2, own_authors, width), BF16),
            vmem((H, 4 * own_authors, width), BF16),
            vmem((H, n_pcol, own_papers, 4 * own_authors), BF16),
            vmem((2, H, own_authors, papers), BF16),
            vmem((nf, G, 2, own_papers, fc), F32),
            vmem((nf, G, own_papers, fc), BF16),
            vmem((nf, G, own_papers, fc), BF16),
            vmem((nf, G, own_papers, fc), BF16),
            vmem((gx, nf, G, own_papers, fc), BF16),
            vmem((nf, 2, G, own_papers, fc), BF16),
            vmem((own_papers, width), BF16),
            vmem((nf, H, own_authors, fc), BF16),
            vmem((nf, H, own_authors, fc), BF16),
            vmem((nf, H, own_authors, fc), F32),
            vmem((nf, H, own_authors, fc), BF16),
            vmem((nf, H, own_authors, fc), BF16),
            vmem((own_authors, width), F32),
            dma((6,)),
            dma((2, hz, 2)), dma((2, hz, 2)), dma((3, hz, 2)), dma((3, hz, 2)),
            dma((nf,)), dma((nf,)), dma((gx, nf)), dma((gx, nf)), dma((nf,)), dma((nf,)),
            dma((nf, H)), dma((nf, H)), dma((nf, H)), dma((nf, H)),
        ],
        compiler_params=pltpu.CompilerParams(
            collective_id=0, has_side_effects=True, vmem_limit_bytes=60 * 1024 * 1024
        ),
    )(tab, author_x, paper_x, w_self, w_rel, w_two, block_vals.reshape(slots, side, side))


def solution(mesh):
    return jax.shard_map(
        functools.partial(per_device, mesh.shape["prow"], mesh.shape["pcol"]),
        mesh=mesh,
        in_specs=(
            P(("prow", "pcol"), None),
            P(("pcol", "prow"), None),
            P(),
            P(),
            P(),
            P("prow", "pcol", None),
            P("prow", "pcol", None),
            P("prow", "pcol", None),
            P("prow", "pcol"),
            P("prow", "pcol", None, None, None),
        ),
        out_specs=(P(("prow", "pcol"), None), P(("pcol", "prow"), None)),
        check_vma=False,
    )
```

time: 79.6 us -> 68.5 us (0.86)
  Pallas kernels: 73.3 us -> 62.3 us
    pallas_call x1, Pallas kernels: 73.3 us -> 62.3 us  [per_device(): pl.pallas_call(functools.partial(kernel, n_prow, n_pcol, wide, fc), out_s...]
where the time goes in v1:
time: 68.5 us; the launch traced here: 68.3 us
  Pallas kernels  62.3 us (91%)
  local copies, waits for them, and re-layouts  3.38 us (5%)
  other arithmetic  1.37 us (2%)
  between operations  1.3 us (2%)
    pallas_call x1, Pallas kernels, per_device(): pl.pallas_call(functools.partial(kernel, n_prow, n_pcol, wide, fc), out_s...  62.3 us
    unnamed x2, local copies, waits for them, and re-layouts  3.38 us

profile of v1, /device:TPU:0, one launch (start us, length us, event | category | flops | bytes accessed | tf_op | source)
XLA Modules:
  0.0 68.3 jit_solution(11111281081973783336)
XLA Ops:
  1.3 0.7 %add_bitcast_fusion.1 = (s32[32]{0:T(128)S(1)}, s32[32]{0:T(128)S(1)}) fusion(s32[1,1,32]{2,1,0:T(1,128)} %param.17, s32[1,1,32]{2,1,0:T(1,128)} %param.16, s32[1,1,32]{2,1,0:T(1,128)} %param.15), kind=kLoop, calls=%fused_computation.6 | loop fusion | flops 96 | bytes 640 | tf_op jit(solution)/shard_map/sub | solution.py:347
  2.0 0.1 select_reduce_fusion.1
  2.1 0.6 pad_add_fusion.tab
  2.7 62.3 %shard_map.113 = (bf16[256,768]{1,0:T(8,128)(2,1)}, bf16[128,768]{1,0:T(8,128)(2,1)}) custom-call(s32[2,64]{1,0:T(2,128)} %pad_add_fusion.tab, bf16[128,768]{1,0:T(8,128)(2,1)} %author_h.1, bf16[256,768]{1,0:T(8,128)(2,1)} %paper_h.1, bf16[768,768]{1,0:T(8,128)(2,1)} %w_self_h.1, bf16[2,768,768]{2,1,0:T(8,128)(2,1)} %w_rel_h.1, bf16[768,768]{1,0:T(8,128)(2,1)} %w_two_h.1, ...), custom_call_target="tpu_custom_call" | custom-call | tf_op jit(solution)/shard_map/pallas_call | solution.py:353
  64.9 1.8 %copy.15 = bf16[256,768]{1,0:T(8,128)(2,1)} copy(bf16[256,768]{1,0:T(8,128)(2,1)} %get-tuple-element.8) | data formatting | bytes 786432
  66.7 1.6 %copy.16 = bf16[128,768]{1,0:T(8,128)(2,1)} copy(bf16[128,768]{1,0:T(8,128)(2,1)} %get-tuple-element.9) | data formatting | bytes 393216
  (2 shorter events, 0.0 us)

commit v2 on v1

--- a/solution.py
+++ b/solution.py
@@ -18,11 +18,11 @@
 
 def kernel(
     n_prow, n_pcol, wide, fc,
-    tab, author_h, paper_h, w_self_h, w_rel_h, w_two_h, blocks_h,
-    hidden_h, author_out,
-    paper, w_self, w_rel, w_two, blocks,
+    rows_h, cols_h, type_h, count_h, author_h, paper_h, w_self_h, w_rel_h, w_two_h, blocks_h,
+    hidden, author_out,
+    rows, columns, types, count, tab_v, tab, paper, w_self, w_rel, w_two, blocks,
     x_all, msgs, dense, dense_t, acc,
-    pair_out, pair_in, x_out, x_in, h_all, hidden,
+    pair_out, pair_in, x_out, x_in, h_all,
     y_out, y_in, y_acc, z_out, z_in, out_acc,
     local_sem,
     g_send, g_recv, gy_send, gy_recv,
@@ -81,20 +81,19 @@
             pl.when(cond)(go)
 
     up_z, down_z = z < H - 1, z > 0
+    peers = 1 + G + up_z.astype(jnp.int32) + down_z.astype(jnp.int32)
     greet(up_z, i + 2, j)
     greet(down_z, i - 2, j)
     greet(None, y_part, j)
     for d in range(1, G):
         greet(None, i, lax.rem(x + d, G) * 2 + c)
     greet(None, i, c_part)
-    for d in range(2, H):
-        greet(z + d <= H - 1, i + 2 * d, j)
-        greet(z - d >= 0, i - 2 * d, j)
 
     loads = [
         pltpu.make_async_copy(src, dst, local_sem.at[n])
         for n, (src, dst) in enumerate(
             (
+                (rows_h, rows), (cols_h, columns), (type_h, types), (count_h, count),
                 (blocks_h, blocks), (w_rel_h, w_rel), (paper_h, paper), (w_self_h, w_self), (w_two_h, w_two),
                 (author_h, x_all.at[z, y]),
             )
@@ -103,7 +102,7 @@
     for load in loads:
         load.start()
 
-    pl.semaphore_wait(barrier, 1 + G + H - 1)
+    pl.semaphore_wait(barrier, peers)
 
     parts = g_send.shape[2]
     part_rows = own_authors // parts
@@ -117,8 +116,24 @@
         send(down_z, mine, piece(z, y, h), g_send.at[1, 0, h], g_recv.at[1, 0, h], i - 2, j)
         send(None, mine, piece(z, y, h), gy_send.at[2, 0, h], gy_recv.at[2, 0, h], y_part, j)
 
-    loads[0].wait()
     row_blocks, col_blocks = papers // side, authors // side
+    for load in loads[:4]:
+        load.wait()
+    place = lax.broadcasted_iota(jnp.int32, (1, tab.shape[1]), 1)
+    which = jnp.zeros_like(place)
+    sort = jnp.full_like(place, 2)
+    for slot in range(blocks.shape[0]):
+        live = jnp.where(slot < count[0, 0], 1, 0)
+        there = rows[0, slot] * col_blocks + columns[0, slot] + (1 - live) * tab.shape[1]
+        here = place == there
+        which = jnp.where(here, slot, which)
+        sort = jnp.where(here, types[0, slot], sort)
+    tab_v[0:1] = which
+    tab_v[1:2] = sort
+    table_copy = pltpu.make_async_copy(tab_v, tab, local_sem.at[0])
+    table_copy.start()
+    table_copy.wait()
+    loads[4].wait()
     p_step, a_step, pair_step = min(side, own_papers), min(side, own_authors), min(side, pair_authors)
 
     def densify(first, last):
@@ -197,7 +212,7 @@
     densify(0, half)
     z_arrival(0)
     densify(half, row_blocks)
-    for load in loads[1:]:
+    for load in loads[5:]:
         load.wait()
     for h in range(parts):
         arrive(piece(z, 1 - y, h), gy_send.at[2, 0, h], gy_recv.at[2, 0, h])
@@ -305,15 +320,12 @@
             to_z(f - 1)
         if f >= 4:
             finish(f - 4)
-    store = pltpu.make_async_copy(hidden, hidden_h, local_sem.at[0])
-    store.start()
     for f in range(max(nf - 4, 0), nf - 2):
         finish(f)
     to_z(nf - 1)
     for f in range(max(nf - 2, 0), nf):
         finish(f)
     author_out[...] = out_acc[...].astype(BF16)
-    store.wait()
 
     for cond, desc in waits:
         if cond is None:
@@ -322,6 +334,17 @@
             @pl.when(cond)
             def _():
                 desc().wait_send()
+
+
+def write_out(hidden, author_out, hidden_h, author_h, sems):
+    stores = [
+        pltpu.make_async_copy(src, dst, sems.at[n])
+        for n, (src, dst) in enumerate(((hidden, hidden_h), (author_out, author_h)))
+    ]
+    for store in stores:
+        store.start()
+    for store in stores:
+        store.wait()
 
 
 def per_device(
@@ -334,32 +357,27 @@
     papers, authors = own_papers * n_pcol, own_authors * n_prow
     col_blocks = authors // side
     places = (papers // side) * col_blocks
+    lanes = (places + 127) // 128 * 128
     H, G = n_prow // 2, n_pcol // 2
     wide = 256 if width % 256 == 0 else 128
     fc = 128
     nf = width // fc
 
-    slot = jnp.arange(slots, dtype=jnp.int32)
-    where = block_rows.reshape(slots) * col_blocks + block_cols.reshape(slots)
-    live = slot < block_count.reshape(())
-    hit = (where[:, None] == jnp.arange(places, dtype=jnp.int32)[None, :]) & live[:, None]
-    which = jnp.sum(jnp.where(hit, slot[:, None], 0), axis=0)
-    kind = 2 + jnp.sum(jnp.where(hit, block_type.reshape(slots)[:, None] - 2, 0), axis=0)
-    tab = jnp.stack([which, kind]).astype(jnp.int32)
-
     vmem, anyspace, smem = pltpu.VMEM, pl.ANY, pltpu.SMEM
     dma = pltpu.SemaphoreType.DMA
     hz, gx = max(H - 1, 1), max(G - 1, 1)
-    return pl.pallas_call(
+    results = pl.pallas_call(
         functools.partial(kernel, n_prow, n_pcol, wide, fc),
-        out_shape=(
-            jax.ShapeDtypeStruct((own_papers, width), BF16),
-            jax.ShapeDtypeStruct((own_authors, width), BF16),
-        ),
-        in_specs=[pl.BlockSpec(memory_space=smem)]
-        + [pl.BlockSpec(memory_space=anyspace)] * 6,
-        out_specs=(pl.BlockSpec(memory_space=anyspace), pl.BlockSpec(memory_space=vmem)),
+        out_shape=(vmem((own_papers, width), BF16), vmem((own_authors, width), BF16)),
+        in_specs=[pl.BlockSpec(memory_space=pltpu.HBM)] * 10,
+        out_specs=(pl.BlockSpec(memory_space=vmem),) * 2,
         scratch_shapes=[
+            smem((1, slots), jnp.int32),
+            smem((1, slots), jnp.int32),
+            smem((1, slots), jnp.int32),
+            smem((1, 1), jnp.int32),
+            vmem((2, lanes), jnp.int32),
+            smem((2, lanes), jnp.int32),
             vmem((own_papers, width), BF16),
             vmem((width, width), BF16),
             vmem(w_rel.shape, BF16),
@@ -375,14 +393,13 @@
             vmem((nf, G, own_papers, fc), BF16),
             vmem((gx, nf, G, own_papers, fc), BF16),
             vmem((nf, 2, G, own_papers, fc), BF16),
-            vmem((own_papers, width), BF16),
             vmem((nf, H, own_authors, fc), BF16),
             vmem((nf, H, own_authors, fc), BF16),
             vmem((nf, H, own_authors, fc), F32),
             vmem((nf, H, own_authors, fc), BF16),
             vmem((nf, H, own_authors, fc), BF16),
             vmem((own_authors, width), F32),
-            dma((6,)),
+            dma((10,)),
             dma((2, hz, 2)), dma((2, hz, 2)), dma((3, hz, 2)), dma((3, hz, 2)),
             dma((nf,)), dma((nf,)), dma((gx, nf)), dma((gx, nf)), dma((nf,)), dma((nf,)),
             dma((nf, H)), dma((nf, H)), dma((nf, H)), dma((nf, H)),
@@ -390,7 +407,20 @@
         compiler_params=pltpu.CompilerParams(
             collective_id=0, has_side_effects=True, vmem_limit_bytes=60 * 1024 * 1024
         ),
-    )(tab, author_x, paper_x, w_self, w_rel, w_two, block_vals.reshape(slots, side, side))
+    )(
+        block_rows.reshape(1, slots), block_cols.reshape(1, slots), block_type.reshape(1, slots), block_count,
+        author_x, paper_x, w_self, w_rel, w_two, block_vals.reshape(slots, side, side),
+    )
+    return pl.pallas_call(
+        write_out,
+        out_shape=(
+            jax.ShapeDtypeStruct((own_papers, width), BF16),
+            jax.ShapeDtypeStruct((own_authors, width), BF16),
+        ),
+        in_specs=[pl.BlockSpec(memory_space=vmem)] * 2,
+        out_specs=(pl.BlockSpec(memory_space=anyspace),) * 2,
+        scratch_shapes=[dma((2,))],
+    )(*[pltpu.with_memory_space_constraint(r, pltpu.VMEM) for r in results])
 
 
 def solution(mesh):

time: 68.5 us -> 62.8 us (0.917)
  local copies, waits for them, and re-layouts: 3.38 us -> 0 us
  other arithmetic: 1.37 us -> 0 us
  Pallas kernels: 62.3 us -> 61.3 us
    unnamed x2 -> x0, local copies, waits for them, and re-layouts: 3.38 us -> none
    pallas_call x1, Pallas kernels: 62.3 us -> 60.5 us  [per_device(): pl.pallas_call(functools.partial(kernel, n_prow, n_pcol, wide, fc), out_s...]
    pallas_call x0 -> x1, Pallas kernels: none -> 0.83 us  [per_device(): pl.pallas_call(write_out, out_shape=(jax.ShapeDtypeStruct((own_papers, wi...]
    sub x1 -> x0, other arithmetic: 0.69 us -> none  [per_device(): block_type.reshape(slots)[:, None] - 2]
where the time goes in v2:
time: 62.8 us; the launch traced here: 62.6 us
  Pallas kernels  61.3 us (98%)
  between operations  1.29 us (2%)
    pallas_call x1, Pallas kernels, per_device(): pl.pallas_call(functools.partial(kernel, n_prow, n_pcol, wide, fc), out_s...  60.5 us

profile of v2, /device:TPU:0, one launch (start us, length us, event | category | flops | bytes accessed | tf_op | source)
XLA Modules:
  0.0 62.6 jit_solution(3445759083901801787)
XLA Ops:
  1.3 60.5 %shard_map.113 = (bf16[256,768]{1,0:T(8,128)(2,1)S(1)}, bf16[128,768]{1,0:T(8,128)(2,1)S(1)}) custom-call(s32[1,32]{1,0:T(1,128)} %bitcast.5, s32[1,32]{1,0:T(1,128)} %bitcast.6, s32[1,32]{1,0:T(1,128)} %bitcast.7, s32[1,1]{1,0:T(1,128)S(6)} %copy.12.count_h, bf16[128,768]{1,0:T(8,128)(2,1)} %author_h.1, bf16[256,768]{1,0:T(8,128)(2,1)} %paper_h.1, ...), custom_call_target="tpu_custom_call" | custom-call | tf_op jit(solution)/shard_map/pallas_call | solution.py:369
  61.8 0.8 %shard_map.114 = (bf16[256,768]{1,0:T(8,128)(2,1)}, bf16[128,768]{1,0:T(8,128)(2,1)}) custom-call(bf16[256,768]{1,0:T(8,128)(2,1)S(1)} %get-tuple-element.4.hidden, bf16[128,768]{1,0:T(8,128)(2,1)S(1)} %get-tuple-element.5.author_out), custom_call_target="tpu_custom_call" | custom-call | tf_op jit(solution)/shard_map/pallas_call | solution.py:414

commit v3 on v2

--- a/solution.py
+++ b/solution.py
@@ -208,10 +208,8 @@
             arrive(piece(near, 1 - y, h), gy_send.at[way, dist - 1, h], gy_recv.at[way, dist - 1, h])
         return near
 
-    half = row_blocks // 2
-    densify(0, half)
+    densify(0, row_blocks)
     z_arrival(0)
-    densify(half, row_blocks)
     for load in loads[5:]:
         load.wait()
     for h in range(parts):
@@ -280,8 +278,8 @@
         near = dot(dense_t[y].reshape(H * own_authors, papers), table)
         y_acc[f] = near.reshape(H, own_authors, fc)
 
-    def to_z(f):
-        for k in range(H):
+    def to_z(f, k_from, k_to):
+        for k in range(k_from, k_to):
             b = target(k)
             arrive(y_in.at[f, b], ys.at[f, b], yr.at[f, b])
             total = y_acc[f, b] + y_in[f, b].astype(F32)
@@ -313,17 +311,24 @@
     for p in range(per):
         to_x((nb - 1) * per + p)
 
+    half = H // 2
     for f in range(nf):
         from_x(f)
+        if f >= 2:
+            to_z(f - 2, half, H)
         to_y(f)
         if f >= 1:
-            to_z(f - 1)
+            to_z(f - 1, 0, half)
         if f >= 4:
             finish(f - 4)
-    for f in range(max(nf - 4, 0), nf - 2):
-        finish(f)
-    to_z(nf - 1)
-    for f in range(max(nf - 2, 0), nf):
+    done = max(nf - 4, 0)
+    if nf > 1:
+        to_z(nf - 2, half, H)
+    if done < nf - 3:
+        finish(done)
+        done += 1
+    to_z(nf - 1, 0, H)
+    for f in range(done, nf):
         finish(f)
     author_out[...] = out_acc[...].astype(BF16)
 

time: 62.8 us -> 60.3 us (0.960)
  Pallas kernels: 61.3 us -> 58.9 us
    pallas_call x1, Pallas kernels: 60.5 us -> 58 us  [per_device(): pl.pallas_call(functools.partial(kernel, n_prow, n_pcol, wide, fc), out_s...]
where the time goes in v3:
time: 60.3 us; the launch traced here: 60.2 us
  Pallas kernels  58.9 us (98%)
  between operations  1.29 us (2%)
    pallas_call x1, Pallas kernels, per_device(): pl.pallas_call(functools.partial(kernel, n_prow, n_pcol, wide, fc), out_s...  58 us

profile of v3, /device:TPU:0, one launch (start us, length us, event | category | flops | bytes accessed | tf_op | source)
XLA Modules:
  0.0 60.2 jit_solution(13750360764375997886)
XLA Ops:
  1.3 58.0 %shard_map.113 = (bf16[256,768]{1,0:T(8,128)(2,1)S(1)}, bf16[128,768]{1,0:T(8,128)(2,1)S(1)}) custom-call(s32[1,32]{1,0:T(1,128)} %bitcast.5, s32[1,32]{1,0:T(1,128)} %bitcast.6, s32[1,32]{1,0:T(1,128)} %bitcast.7, s32[1,1]{1,0:T(1,128)S(6)} %copy.12.count_h, bf16[128,768]{1,0:T(8,128)(2,1)} %author_h.1, bf16[256,768]{1,0:T(8,128)(2,1)} %paper_h.1, ...), custom_call_target="tpu_custom_call" | custom-call | tf_op jit(solution)/shard_map/pallas_call | solution.py:374
  59.3 0.8 %shard_map.114 = (bf16[256,768]{1,0:T(8,128)(2,1)}, bf16[128,768]{1,0:T(8,128)(2,1)}) custom-call(bf16[256,768]{1,0:T(8,128)(2,1)S(1)} %get-tuple-element.4.hidden, bf16[128,768]{1,0:T(8,128)(2,1)S(1)} %get-tuple-element.5.author_out), custom_call_target="tpu_custom_call" | custom-call | tf_op jit(solution)/shard_map/pallas_call | solution.py:419

commit v4 on v3

--- a/solution.py
+++ b/solution.py
@@ -63,6 +63,16 @@
                 desc().start()
         waits.append((cond, desc))
 
+    def settle(count):
+        for cond, desc in waits[:count]:
+            if cond is None:
+                desc().wait_send()
+            else:
+                @pl.when(cond)
+                def _():
+                    desc().wait_send()
+        del waits[:count]
+
     def arrive(dst, ss, rs):
         pltpu.make_async_remote_copy(
             src_ref=dst, dst_ref=dst, send_sem=ss, recv_sem=rs,
@@ -156,7 +166,11 @@
                 flip = (block * (kind < 2).astype(F32)).T.astype(BF16)
                 for sub in range(side // a_step):
                     owner = (cb * side + sub * a_step) // own_authors
-                    dense_t[owner % 2, owner // 2, :, rb * side:(rb + 1) * side] = flip[sub * a_step:(sub + 1) * a_step]
+                    for lane in range(side // p_step):
+                        row = rb * side + lane * p_step
+                        dense_t[
+                            row // own_papers, owner % 2, owner // 2, :, row % own_papers:row % own_papers + p_step,
+                        ] = flip[sub * a_step:(sub + 1) * a_step, lane * p_step:(lane + 1) * p_step]
 
     def z_arrival(s):
         for h in range(parts):
@@ -227,6 +241,7 @@
         slab(from_y(k), False)
         if k + 2 <= H - 2:
             z_arrival(k + 2)
+    gathered = len(waits)
     last = from_y(H - 2)
 
     def to_pair(n):
@@ -265,33 +280,55 @@
     def target(k):
         return jnp.where(low, H - 1 - k, k)
 
+    start = jnp.where(low, H - H // 2, 0)
+    other = jnp.where(low, 0, H // 2)
+
+    def half_sum(f, yy, at, count, core):
+        total = None
+        for b in range(G):
+            part = dot(
+                dense_t[b * 2 + core, yy, pl.ds(at, count)].reshape(count * own_authors, own_papers), h_all[f, core, b]
+            )
+            total = part if total is None else total + part
+        return total.reshape(count, own_authors, fc)
+
+    spans = ((start, H // 2, 0), (other, H - H // 2, H // 2))
+
+    def rows_of(f):
+        split = 1
+        step = own_authors // split
+        return [(p, pl.ds(p * step, step)) for p in range(split)]
+
     def to_y(f):
+        for at, count, _ in spans:
+            y_acc[f, pl.ds(at, count)] = half_sum(f, 1 - y, at, count, c)
         arrive(h_all.at[f, 1 - c], hs.at[f], hr.at[f])
-        table = jnp.concatenate(
-            [h_all[f, q % 2, q // 2] for q in range(n_pcol)], axis=0
-        )
-        far = dot(dense_t[1 - y].reshape(H * own_authors, papers), table)
-        y_out[f] = far.astype(BF16).reshape(H, own_authors, fc)
-        for k in range(H):
-            b = target(k)
-            send(None, y_out.at[f, b], y_in.at[f, b], ys.at[f, b], yr.at[f, b], y_part, j)
-        near = dot(dense_t[y].reshape(H * own_authors, papers), table)
-        y_acc[f] = near.reshape(H, own_authors, fc)
+        for at, count, k_from in spans:
+            far = y_acc[f, pl.ds(at, count)] + half_sum(f, 1 - y, at, count, 1 - c)
+            y_out[f, pl.ds(at, count)] = far.astype(BF16)
+            for k in range(k_from, k_from + count):
+                b = target(k)
+                for p, rows in rows_of(f):
+                    send(None, y_out.at[f, b, rows], y_in.at[f, b, rows], ys.at[f, b, p], yr.at[f, b, p], y_part, j)
+        for at, count, _ in spans:
+            y_acc[f, pl.ds(at, count)] = half_sum(f, y, at, count, c) + half_sum(f, y, at, count, 1 - c)
 
     def to_z(f, k_from, k_to):
         for k in range(k_from, k_to):
             b = target(k)
-            arrive(y_in.at[f, b], ys.at[f, b], yr.at[f, b])
-            total = y_acc[f, b] + y_in[f, b].astype(F32)
-            y_acc[f, b] = total
-            z_out[f, b] = total.astype(BF16)
-            send(b != z, z_out.at[f, b], z_in.at[f, z], zs.at[f, b], zr.at[f, z], b * 2 + y, j)
+            for p, rows in rows_of(f):
+                arrive(y_in.at[f, b, rows], ys.at[f, b, p], yr.at[f, b, p])
+                total = y_acc[f, b, rows] + y_in[f, b, rows].astype(F32)
+                y_acc[f, b, rows] = total
+                z_out[f, b, rows] = total.astype(BF16)
+                send(b != z, z_out.at[f, b, rows], z_in.at[f, z, rows], zs.at[f, b, p], zr.at[f, z, p], b * 2 + y, j)
 
     def finish(f):
         for s in range(H):
             @pl.when(z != s)
             def _():
-                arrive(z_in.at[f, s], zs.at[f, s], zr.at[f, s])
+                for p, rows in rows_of(f):
+                    arrive(z_in.at[f, s, rows], zs.at[f, s, p], zr.at[f, s, p])
                 y_acc[f, z] = y_acc[f, z] + z_in[f, s].astype(F32)
 
         total = y_acc[f, z]
@@ -303,17 +340,23 @@
             value = dot(high, weight) + dot(rest, weight)
             out_acc[:, cols] = value if f == 0 else out_acc[:, cols] + value
 
-    for n in range(nb):
+    to_pair(0)
+    for p in range(per):
+        to_x(p)
+    for n in range(1, nb):
         to_pair(n)
-        if n > 0:
+        if n > 1:
             for p in range(per):
                 to_x((n - 1) * per + p)
     for p in range(per):
         to_x((nb - 1) * per + p)
 
+    settle(gathered)
     half = H // 2
     for f in range(nf):
         from_x(f)
+        if f == nf - 1:
+            sent = len(waits)
         if f >= 2:
             to_z(f - 2, half, H)
         to_y(f)
@@ -328,17 +371,12 @@
         finish(done)
         done += 1
     to_z(nf - 1, 0, H)
+    settle(sent)
     for f in range(done, nf):
         finish(f)
     author_out[...] = out_acc[...].astype(BF16)
 
-    for cond, desc in waits:
-        if cond is None:
-            desc().wait_send()
-        else:
-            @pl.when(cond)
-            def _():
-                desc().wait_send()
+    settle(len(waits))
 
 
 def write_out(hidden, author_out, hidden_h, author_h, sems):
@@ -391,7 +429,7 @@
             vmem((H, 2, own_authors, width), BF16),
             vmem((H, 4 * own_authors, width), BF16),
             vmem((H, n_pcol, own_papers, 4 * own_authors), BF16),
-            vmem((2, H, own_authors, papers), BF16),
+            vmem((n_pcol, 2, H, own_authors, own_papers), BF16),
             vmem((nf, G, 2, own_papers, fc), F32),
             vmem((nf, G, own_papers, fc), BF16),
             vmem((nf, G, own_papers, fc), BF16),
@@ -407,7 +445,7 @@
             dma((10,)),
             dma((2, hz, 2)), dma((2, hz, 2)), dma((3, hz, 2)), dma((3, hz, 2)),
             dma((nf,)), dma((nf,)), dma((gx, nf)), dma((gx, nf)), dma((nf,)), dma((nf,)),
-            dma((nf, H)), dma((nf, H)), dma((nf, H)), dma((nf, H)),
+            dma((nf, H, 2)), dma((nf, H, 2)), dma((nf, H, 2)), dma((nf, H, 2)),
         ],
         compiler_params=pltpu.CompilerParams(
             collective_id=0, has_side_effects=True, vmem_limit_bytes=60 * 1024 * 1024

time: 60.3 us -> 59.7 us (0.990)
  Pallas kernels: 58.9 us -> 58.1 us
    pallas_call x1, Pallas kernels: 58 us -> 57.3 us  [per_device(): pl.pallas_call(functools.partial(kernel, n_prow, n_pcol, wide, fc), out_s...]
where the time goes in v4:
time: 59.7 us; the launch traced here: 59.5 us
  Pallas kernels  58.1 us (97%)
  between operations  1.45 us (2%)
    pallas_call x1, Pallas kernels, per_device(): pl.pallas_call(functools.partial(kernel, n_prow, n_pcol, wide, fc), out_s...  57.3 us

profile of v4, /device:TPU:0, one launch (start us, length us, event | category | flops | bytes accessed | tf_op | source)
XLA Modules:
  0.0 59.5 jit_solution(18121030980986732486)
XLA Ops:
  1.3 57.3 %shard_map.113 = (bf16[256,768]{1,0:T(8,128)(2,1)S(1)}, bf16[128,768]{1,0:T(8,128)(2,1)S(1)}) custom-call(s32[1,32]{1,0:T(1,128)} %bitcast.5, s32[1,32]{1,0:T(1,128)} %bitcast.6, s32[1,32]{1,0:T(1,128)} %bitcast.7, s32[1,1]{1,0:T(1,128)S(6)} %copy.12.count_h, bf16[128,768]{1,0:T(8,128)(2,1)} %author_h.1, bf16[256,768]{1,0:T(8,128)(2,1)} %paper_h.1, ...), custom_call_target="tpu_custom_call" | custom-call | tf_op jit(solution)/shard_map/pallas_call | solution.py:412
  58.5 0.8 %shard_map.114 = (bf16[256,768]{1,0:T(8,128)(2,1)}, bf16[128,768]{1,0:T(8,128)(2,1)}) custom-call(bf16[256,768]{1,0:T(8,128)(2,1)S(1)} %get-tuple-element.4.hidden, bf16[128,768]{1,0:T(8,128)(2,1)S(1)} %get-tuple-element.5.author_out), custom_call_target="tpu_custom_call" | custom-call | tf_op jit(solution)/shard_map/pallas_call | solution.py:457

commit v5 on v4

--- a/solution.py
+++ b/solution.py
@@ -362,12 +362,10 @@
         to_y(f)
         if f >= 1:
             to_z(f - 1, 0, half)
-        if f >= 4:
-            finish(f - 4)
-    done = max(nf - 4, 0)
+    done = 0
     if nf > 1:
         to_z(nf - 2, half, H)
-    if done < nf - 3:
+    while done < nf - 3:
         finish(done)
         done += 1
     to_z(nf - 1, 0, H)

time: 59.7 us -> 59.5 us (level)
  no operation moved by 1% of the time
where the time goes in v5:
time: 59.5 us; the launch traced here: 59.3 us
  Pallas kernels  57.9 us (97%)
  between operations  1.45 us (2%)
    pallas_call x1, Pallas kernels, per_device(): pl.pallas_call(functools.partial(kernel, n_prow, n_pcol, wide, fc), out_s...  57.1 us

profile of v5, /device:TPU:0, one launch (start us, length us, event | category | flops | bytes accessed | tf_op | source)
XLA Modules:
  0.0 59.3 jit_solution(10023061786285348312)
XLA Ops:
  1.3 57.1 %shard_map.113 = (bf16[256,768]{1,0:T(8,128)(2,1)S(1)}, bf16[128,768]{1,0:T(8,128)(2,1)S(1)}) custom-call(s32[1,32]{1,0:T(1,128)} %bitcast.5, s32[1,32]{1,0:T(1,128)} %bitcast.6, s32[1,32]{1,0:T(1,128)} %bitcast.7, s32[1,1]{1,0:T(1,128)S(6)} %copy.12.count_h, bf16[128,768]{1,0:T(8,128)(2,1)} %author_h.1, bf16[256,768]{1,0:T(8,128)(2,1)} %paper_h.1, ...), custom_call_target="tpu_custom_call" | custom-call | tf_op jit(solution)/shard_map/pallas_call | solution.py:410
  58.3 0.8 %shard_map.114 = (bf16[256,768]{1,0:T(8,128)(2,1)}, bf16[128,768]{1,0:T(8,128)(2,1)}) custom-call(bf16[256,768]{1,0:T(8,128)(2,1)S(1)} %get-tuple-element.4.hidden, bf16[128,768]{1,0:T(8,128)(2,1)S(1)} %get-tuple-element.5.author_out), custom_call_target="tpu_custom_call" | custom-call | tf_op jit(solution)/shard_map/pallas_call | solution.py:455
